TPU v7x, 256 devices: a whole 4x4x8 slice. The times are simulated.
256 devices in a mesh: blk: 16 (over z_hi, y), grp: 16 (over z_lo, x, core).
Axes of the slice: x: 4, y: 4, z: 8 (z_hi: 4, z_lo: 2; z = z_hi * 2 + z_lo), core: 2. Of those that a mesh axis runs over, the one named last changes fastest.
Arguments:
- tiles: bfloat16 [1024, 20, 128, 128], P(('blk', 'grp')), may hold values from -1 to 3.5
- columns: int32 [1024, 20], P(('blk', 'grp')), may hold values from -1 to 1023, as said below
Outputs:
- square: bfloat16 [1024, 20, 128, 128], P(('blk', 'grp'))
- trace_mean: float32 [], replicated
Inputs may be any that keep to these rules, and one draw needn't show every extreme that they name: Slot 0 of row i holds i. The filled slots of a row come first, then -1. The filled columns of a row are distinct and lie within 12 block rows of i, counted periodically modulo 1024. Every device has a row with all 20 slots filled that reaches i - 12 and one that reaches i + 12.
All inputs are finite; a program needn't handle non-finite values.
Results may differ from a plain program's by a relative error of at most 0.001.
Values may be sent and summed in bfloat16 or wider, within the bound.
A program may use at most 192 MiB of HBM per device.

v0:
```python
import jax
import jax.numpy as jnp
from jax import lax
from jax.sharding import PartitionSpec as P

REACH = 12


def shifted(shard, axis, by):
    size = lax.axis_size(axis)
    return lax.ppermute(shard, axis, [(i, (i + by) % size) for i in range(size)])


def shards(tiles, columns):
    shard_rows = tiles.shape[0]
    slots_count = tiles.shape[1]
    block_size = tiles.shape[2]
    devices = lax.axis_size(("blk", "grp"))
    all_rows = shard_rows * devices
    device = lax.axis_index(("blk", "grp"))
    hop_count = (REACH + shard_rows - 1) // shard_rows
    window_count = 2 * hop_count + 1
    tile_buf = jnp.zeros((window_count,) + tiles.shape, tiles.dtype).at[hop_count].set(tiles)
    col_buf = jnp.zeros((window_count,) + columns.shape, jnp.int32).at[hop_count].set(columns)

    def advance(hop_step, loop_state):
        lower_piece, upper_piece, tile_acc, col_acc = loop_state
        lower_piece = shifted((lower_piece[0], lower_piece[1]), ("blk", "grp"), 1)
        upper_piece = shifted((upper_piece[0], upper_piece[1]), ("blk", "grp"), -1)
        below_slot = hop_count - 1 - hop_step
        above_slot = hop_count + 1 + hop_step
        tile_acc = lax.dynamic_update_index_in_dim(tile_acc, lower_piece[0], below_slot, 0)
        col_acc = lax.dynamic_update_index_in_dim(col_acc, lower_piece[1], below_slot, 0)
        tile_acc = lax.dynamic_update_index_in_dim(tile_acc, upper_piece[0], above_slot, 0)
        col_acc = lax.dynamic_update_index_in_dim(col_acc, upper_piece[1], above_slot, 0)
        return (lower_piece, upper_piece, tile_acc, col_acc)

    start_state = ((tiles, columns), (tiles, columns), tile_buf, col_buf)
    final_state = lax.fori_loop(0, hop_count, advance, start_state)
    window_tiles = final_state[2]
    window_cols = final_state[3]
    row_tiles = window_tiles.reshape(window_count * shard_rows, slots_count, block_size, block_size)
    row_cols = window_cols.reshape(window_count * shard_rows, slots_count)
    first_row = (device - hop_count) * shard_rows

    def one_row(inputs):
        own_tiles, own_cols = inputs
        filled = own_cols >= 0
        position = jnp.where(filled, jnp.mod(own_cols - first_row, all_rows), 0)
        far_tiles = row_tiles[position]
        far_cols = row_cols[position]
        routing = (
            (far_cols[:, :, None] == own_cols[None, None, :])
            & filled[None, None, :]
            & filled[:, None, None]
        ).astype(jnp.bfloat16)
        panel = jnp.einsum(
            "tus,tubc->tsbc", routing, far_tiles, preferred_element_type=jnp.float32
        ).astype(jnp.bfloat16)
        product = jnp.einsum("tab,tsbc->sac", own_tiles, panel, preferred_element_type=jnp.float32)
        return (product.astype(jnp.bfloat16), jnp.trace(product[0]))

    square, traces = lax.map(one_row, (tiles, columns))
    total_trace = lax.psum(jnp.sum(traces), ("blk", "grp"))
    trace_mean = total_trace / (all_rows * block_size)
    return (square, trace_mean)


def solution(mesh):
    return jax.shard_map(
        shards,
        mesh=mesh,
        in_specs=(P(("blk", "grp"), None, None, None), P(("blk", "grp"), None)),
        out_specs=(P(("blk", "grp"), None, None, None), P()),
        check_vma=False,
    )
```

profile of v0, /device:TPU:1, one launch (start us, length us, event | category | flops | bytes accessed | tf_op | source)
XLA Modules:
  0.0 485.5 jit_solution(69121832319572027)
XLA Ops:
  1.3 8.1 %scatter.6 = bf16[7,4,20,128,128]{4,3,2,1,0:T(8,128)(2,1)} pad(bf16[1,4,20,128,128]{4,3,2,1,0:T(8,128)(2,1)} %bitcast.77, bf16[]{:T(256)} %constant.169.clone.1), padding=3_3x0_0x0_0x0_0x0_0 | pad | bytes 20971522 | tf_op jit(solution)/shard_map/scatter | solution.py:23
  12.3 128.6 %while.39 = (s32[]{:T(128)}, bf16[4,20,128,128]{3,2,1,0:T(8,128)(2,1)}, s32[4,20]{1,0:T(4,128)S(1)}, bf16[4,20,128,128]{3,2,1,0:T(8,128)(2,1)}, s32[4,20]{1,0:T(...) while((s32[]{:T(128)}, ...), condition=%wide.region_1.0_spmd, body=%wide.region_0.0_spmd.sunk | while | flops 10 | bytes 41955460 | solution.py:39
  16.7 7.2 %collective-permute-start.3 = (s32[4,20]{1,0:T(4,128)S(1)}, s32[4,20]{1,0:T(4,128)S(1)}, u32[]{:S(2)}, u32[]{:S(2)}) collective-permute-start(s32[4,20]{1,0:T(4,128)S(1)} %get-tuple-element.407), channel_id=1, source_target_pairs={{0,255},{1,0},{2,1},{3,2},{4,3},{5,4},{6,5},{7,6},{8,7},{9,8},{10,... | collective-permute-start | bytes 968 | tf_op jit(solution)/shard_map/while/body/eval_jaxpr/ppermute | solution.py:11
  23.9 20.0 %collective-permute-done.1 = s32[4,20]{1,0:T(4,128)S(1)} collective-permute-done((s32[4,20]{1,0:T(4,128)S(1)}, s32[4,20]{1,0:T(4,128)S(1)}, u32[]{:S(2)}, u32[]{:S(2)}) %collective-permute-start.1) | collective-permute-done | bytes 352 | tf_op jit(solution)/shard_map/while/body/eval_jaxpr/ppermute | solution.py:11
  63.8 7.2 %collective-permute-start.3 = (s32[4,20]{1,0:T(4,128)S(1)}, s32[4,20]{1,0:T(4,128)S(1)}, u32[]{:S(2)}, u32[]{:S(2)}) collective-permute-start(s32[4,20]{1,0:T(4,128)S(1)} %get-tuple-element.407), channel_id=1, source_target_pairs={{0,255},{1,0},{2,1},{3,2},{4,3},{5,4},{6,5},{7,6},{8,7},{9,8},{10,... | collective-permute-start | bytes 968 | tf_op jit(solution)/shard_map/while/body/eval_jaxpr/ppermute | solution.py:11
  71.0 14.9 %collective-permute-done.1 = s32[4,20]{1,0:T(4,128)S(1)} collective-permute-done((s32[4,20]{1,0:T(4,128)S(1)}, s32[4,20]{1,0:T(4,128)S(1)}, u32[]{:S(2)}, u32[]{:S(2)}) %collective-permute-start.1) | collective-permute-done | bytes 352 | tf_op jit(solution)/shard_map/while/body/eval_jaxpr/ppermute | solution.py:11
  99.0 11.9 %collective-permute-start.2 = (bf16[4,20,128,128]{3,2,1,0:T(8,128)(2,1)}, bf16[4,20,128,128]{3,2,1,0:T(8,128)(2,1)S(1)}, u32[]{:S(2)}, u32[]{:S(2)}) collective-permute-start(bf16[4,20,128,128]{3,2,1,0:T(8,128)(2,1)} %get-tuple-element.406), channel_id=1, source_target_pairs={{0,255},{1,0},{2,1},{3,2},{4,3},{5,4},{6,5},{7,6},{8,7},{9,8},{10,... | collective-permute-start | bytes 7864328 | tf_op jit(solution)/shard_map/while/body/eval_jaxpr/ppermute | solution.py:11
  110.9 7.2 %collective-permute-start.3 = (s32[4,20]{1,0:T(4,128)S(1)}, s32[4,20]{1,0:T(4,128)S(1)}, u32[]{:S(2)}, u32[]{:S(2)}) collective-permute-start(s32[4,20]{1,0:T(4,128)S(1)} %get-tuple-element.407), channel_id=1, source_target_pairs={{0,255},{1,0},{2,1},{3,2},{4,3},{5,4},{6,5},{7,6},{8,7},{9,8},{10,... | collective-permute-start | bytes 968 | tf_op jit(solution)/shard_map/while/body/eval_jaxpr/ppermute | solution.py:11
  118.1 9.8 %collective-permute-done.1 = s32[4,20]{1,0:T(4,128)S(1)} collective-permute-done((s32[4,20]{1,0:T(4,128)S(1)}, s32[4,20]{1,0:T(4,128)S(1)}, u32[]{:S(2)}, u32[]{:S(2)}) %collective-permute-start.1) | collective-permute-done | bytes 352 | tf_op jit(solution)/shard_map/while/body/eval_jaxpr/ppermute | solution.py:11
  141.0 247.2 %while.40 = (s32[]{:T(128)}, bf16[4,20,128,128]{3,2,1,0:T(8,128)(2,1)}, f32[4]{0:T(128)S(1)}, s32[4,20]{1,0:T(4,128)S(1)}, s32[]{:T(128)}, /*index=5*/s32[28,20]...) while((s32[]{:T(128)}, bf16[4,20,128,128]{3,2,1,0:T(8,128)(2,1)}, ...), condition=%wide.region_4.5_spmd, body=%wide.region_2.4_spmd.sunk | while | flops 1940267776 | bytes 98380256 | solution.py:63
  141.2 12.7 %gather_fusion = bf16[20,20,128,128]{3,2,1,0:T(8,128)(2,1)} fusion(bf16[28,20,128,128]{3,2,1,0:T(8,128)(2,1)} %get-tuple-element.453, s32[1024]{0:T(1024)S(1)} %pad_clamp_fusion.2), kind=kCustom, calls=%fused_computation.1.clone.1 | custom fusion | bytes 26214480 | tf_op jit(solution)/shard_map/while/body/eval_jaxpr/gather | solution.py:50
  154.5 19.4 %fusion.38 = bf16[20,20,128,128]{3,1,2,0:T(8,128)(2,1)} fusion(bf16[20,20,128,128]{3,2,1,0:T(8,128)(2,1)} %gather_fusion, s32[20]{0:T(128)S(1)} %get-tuple-element.388, s32[20,20]{1,0:T(8,128)S(1)} %gather_fusion.1, pred[20]{0:T(512)(128)(4,1)S(1)} %get-tuple-element.389), kind=kOutput, calls=%fused_computation.6.clone.1 | convolution fusion | flops 262168000 | bytes 26216100 | tf_op jit(solution)/shard_map/while/body/eval_jaxpr/tus,tubc->tsbc/dot_general | solution.py:57
  173.9 19.5 %copy.19 = bf16[20,20,128,128]{2,3,0,1:T(8,128)(2,1)} copy(bf16[20,20,128,128]{3,1,2,0:T(8,128)(2,1)} %fusion.38) | data formatting | bytes 26214400 | tf_op jit(solution)/shard_map/while/body/eval_jaxpr/tus,tubc->tsbc/dot_general | solution.py:57
  203.0 12.7 %gather_fusion = bf16[20,20,128,128]{3,2,1,0:T(8,128)(2,1)} fusion(bf16[28,20,128,128]{3,2,1,0:T(8,128)(2,1)} %get-tuple-element.453, s32[1024]{0:T(1024)S(1)} %pad_clamp_fusion.2), kind=kCustom, calls=%fused_computation.1.clone.1 | custom fusion | bytes 26214480 | tf_op jit(solution)/shard_map/while/body/eval_jaxpr/gather | solution.py:50
  216.3 19.4 %fusion.38 = bf16[20,20,128,128]{3,1,2,0:T(8,128)(2,1)} fusion(bf16[20,20,128,128]{3,2,1,0:T(8,128)(2,1)} %gather_fusion, s32[20]{0:T(128)S(1)} %get-tuple-element.388, s32[20,20]{1,0:T(8,128)S(1)} %gather_fusion.1, pred[20]{0:T(512)(128)(4,1)S(1)} %get-tuple-element.389), kind=kOutput, calls=%fused_computation.6.clone.1 | convolution fusion | flops 262168000 | bytes 26216100 | tf_op jit(solution)/shard_map/while/body/eval_jaxpr/tus,tubc->tsbc/dot_general | solution.py:57
  235.6 19.5 %copy.19 = bf16[20,20,128,128]{2,3,0,1:T(8,128)(2,1)} copy(bf16[20,20,128,128]{3,1,2,0:T(8,128)(2,1)} %fusion.38) | data formatting | bytes 26214400 | tf_op jit(solution)/shard_map/while/body/eval_jaxpr/tus,tubc->tsbc/dot_general | solution.py:57
  255.2 6.9 %fusion.39 = f32[20,128,128]{1,2,0:T(8,128)S(1)} fusion(bf16[20,20,128,128]{2,3,0,1:T(8,128)(2,1)} %copy.19, bf16[4,20,128,128]{3,2,1,0:T(8,128)(2,1)} %get-tuple-element.454, s32[]{:T(128)} %get-tuple-element.438), kind=kOutput, calls=%fused_computation.10.clone.1 | convolution fusion | flops 1677721600 | bytes 15073792 | tf_op jit(solution)/shard_map/while/body/eval_jaxpr/tab,tsbc->sac/dot_general | solution.py:60
  264.8 12.7 %gather_fusion = bf16[20,20,128,128]{3,2,1,0:T(8,128)(2,1)} fusion(bf16[28,20,128,128]{3,2,1,0:T(8,128)(2,1)} %get-tuple-element.453, s32[1024]{0:T(1024)S(1)} %pad_clamp_fusion.2), kind=kCustom, calls=%fused_computation.1.clone.1 | custom fusion | bytes 26214480 | tf_op jit(solution)/shard_map/while/body/eval_jaxpr/gather | solution.py:50
  278.0 19.4 %fusion.38 = bf16[20,20,128,128]{3,1,2,0:T(8,128)(2,1)} fusion(bf16[20,20,128,128]{3,2,1,0:T(8,128)(2,1)} %gather_fusion, s32[20]{0:T(128)S(1)} %get-tuple-element.388, s32[20,20]{1,0:T(8,128)S(1)} %gather_fusion.1, pred[20]{0:T(512)(128)(4,1)S(1)} %get-tuple-element.389), kind=kOutput, calls=%fused_computation.6.clone.1 | convolution fusion | flops 262168000 | bytes 26216100 | tf_op jit(solution)/shard_map/while/body/eval_jaxpr/tus,tubc->tsbc/dot_general | solution.py:57
  297.4 19.5 %copy.19 = bf16[20,20,128,128]{2,3,0,1:T(8,128)(2,1)} copy(bf16[20,20,128,128]{3,1,2,0:T(8,128)(2,1)} %fusion.38) | data formatting | bytes 26214400 | tf_op jit(solution)/shard_map/while/body/eval_jaxpr/tus,tubc->tsbc/dot_general | solution.py:57
  326.5 12.7 %gather_fusion = bf16[20,20,128,128]{3,2,1,0:T(8,128)(2,1)} fusion(bf16[28,20,128,128]{3,2,1,0:T(8,128)(2,1)} %get-tuple-element.453, s32[1024]{0:T(1024)S(1)} %pad_clamp_fusion.2), kind=kCustom, calls=%fused_computation.1.clone.1 | custom fusion | bytes 26214480 | tf_op jit(solution)/shard_map/while/body/eval_jaxpr/gather | solution.py:50
  339.8 19.4 %fusion.38 = bf16[20,20,128,128]{3,1,2,0:T(8,128)(2,1)} fusion(bf16[20,20,128,128]{3,2,1,0:T(8,128)(2,1)} %gather_fusion, s32[20]{0:T(128)S(1)} %get-tuple-element.388, s32[20,20]{1,0:T(8,128)S(1)} %gather_fusion.1, pred[20]{0:T(512)(128)(4,1)S(1)} %get-tuple-element.389), kind=kOutput, calls=%fused_computation.6.clone.1 | convolution fusion | flops 262168000 | bytes 26216100 | tf_op jit(solution)/shard_map/while/body/eval_jaxpr/tus,tubc->tsbc/dot_general | solution.py:57
  359.2 19.5 %copy.19 = bf16[20,20,128,128]{2,3,0,1:T(8,128)(2,1)} copy(bf16[20,20,128,128]{3,1,2,0:T(8,128)(2,1)} %fusion.38) | data formatting | bytes 26214400 | tf_op jit(solution)/shard_map/while/body/eval_jaxpr/tus,tubc->tsbc/dot_general | solution.py:57
  388.8 94.9 %psum.7 = f32[]{:T(128)} all-reduce(f32[]{:T(128)} %reduce_sum.22), channel_id=1, replica_groups=mesh['blk'=16,'grp'=16] {'blk','grp'}, use_global_device_ids=true, to_apply=%region_6.7 | all-reduce | flops 1 | bytes 8 | tf_op jit(solution)/shard_map/psum | solution.py:64
  (93 shorter events, 88.4 us)
Async XLA Ops:
  1.3 8.1 %copy-start = (bf16[4,20,128,128]{3,2,1,0:T(8,128)(2,1)S(1)}, bf16[4,20,128,128]{3,2,1,0:T(8,128)(2,1)}, u32[]{:S(2)}) copy-start(bf16[4,20,128,128]{3,2,1,0:T(8,128)(2,1)} %param.10) | copy-start | bytes 7864324
  10.9 1.5 copy-start.1
  12.3 34.3 %collective-permute-start = (bf16[4,20,128,128]{3,2,1,0:T(8,128)(2,1)}, bf16[4,20,128,128]{3,2,1,0:T(8,128)(2,1)}, u32[]{:S(2)}, u32[]{:S(2)}) collective-permute-start(bf16[4,20,128,128]{3,2,1,0:T(8,128)(2,1)} %get-tuple-element.404), channel_id=1, source_target_pairs={{0,1},{1,2},{2,3},{3,4},{4,5},{5,6},{6,7},{7,8},{8,9},{9,10},{10,1... | collective-permute-start | bytes 7864328 | tf_op jit(solution)/shard_map/while/body/eval_jaxpr/ppermute | solution.py:11
  14.9 38.9 %collective-permute-start.2 = (bf16[4,20,128,128]{3,2,1,0:T(8,128)(2,1)}, bf16[4,20,128,128]{3,2,1,0:T(8,128)(2,1)S(1)}, u32[]{:S(2)}, u32[]{:S(2)}) collective-permute-start(bf16[4,20,128,128]{3,2,1,0:T(8,128)(2,1)} %get-tuple-element.406), channel_id=1, source_target_pairs={{0,255},{1,0},{2,1},{3,2},{4,3},{5,4},{6,5},{7,6},{8,7},{9,8},{10,... | collective-permute-start | bytes 7864328 | tf_op jit(solution)/shard_map/while/body/eval_jaxpr/ppermute | solution.py:11
  15.6 28.2 %collective-permute-start.1 = (s32[4,20]{1,0:T(4,128)S(1)}, s32[4,20]{1,0:T(4,128)S(1)}, u32[]{:S(2)}, u32[]{:S(2)}) collective-permute-start(s32[4,20]{1,0:T(4,128)S(1)} %get-tuple-element.405), channel_id=1, source_target_pairs={{0,1},{1,2},{2,3},{3,4},{4,5},{5,6},{6,7},{7,8},{8,9},{9,10},{10,1... | collective-permute-start | bytes 968 | tf_op jit(solution)/shard_map/while/body/eval_jaxpr/ppermute | solution.py:11
  16.7 30.0 %collective-permute-start.3 = (s32[4,20]{1,0:T(4,128)S(1)}, s32[4,20]{1,0:T(4,128)S(1)}, u32[]{:S(2)}, u32[]{:S(2)}) collective-permute-start(s32[4,20]{1,0:T(4,128)S(1)} %get-tuple-element.407), channel_id=1, source_target_pairs={{0,255},{1,0},{2,1},{3,2},{4,3},{5,4},{6,5},{7,6},{8,7},{9,8},{10,... | collective-permute-start | bytes 968 | tf_op jit(solution)/shard_map/while/body/eval_jaxpr/ppermute | solution.py:11
  57.0 31.7 %collective-permute-start = (bf16[4,20,128,128]{3,2,1,0:T(8,128)(2,1)}, bf16[4,20,128,128]{3,2,1,0:T(8,128)(2,1)}, u32[]{:S(2)}, u32[]{:S(2)}) collective-permute-start(bf16[4,20,128,128]{3,2,1,0:T(8,128)(2,1)} %get-tuple-element.404), channel_id=1, source_target_pairs={{0,1},{1,2},{2,3},{3,4},{4,5},{5,6},{6,7},{7,8},{8,9},{9,10},{10,1... | collective-permute-start | bytes 7864328 | tf_op jit(solution)/shard_map/while/body/eval_jaxpr/ppermute | solution.py:11
  57.0 38.9 %collective-permute-start.2 = (bf16[4,20,128,128]{3,2,1,0:T(8,128)(2,1)}, bf16[4,20,128,128]{3,2,1,0:T(8,128)(2,1)S(1)}, u32[]{:S(2)}, u32[]{:S(2)}) collective-permute-start(bf16[4,20,128,128]{3,2,1,0:T(8,128)(2,1)} %get-tuple-element.406), channel_id=1, source_target_pairs={{0,255},{1,0},{2,1},{3,2},{4,3},{5,4},{6,5},{7,6},{8,7},{9,8},{10,... | collective-permute-start | bytes 7864328 | tf_op jit(solution)/shard_map/while/body/eval_jaxpr/ppermute | solution.py:11
  63.8 22.1 %collective-permute-start.1 = (s32[4,20]{1,0:T(4,128)S(1)}, s32[4,20]{1,0:T(4,128)S(1)}, u32[]{:S(2)}, u32[]{:S(2)}) collective-permute-start(s32[4,20]{1,0:T(4,128)S(1)} %get-tuple-element.405), channel_id=1, source_target_pairs={{0,1},{1,2},{2,3},{3,4},{4,5},{5,6},{6,7},{7,8},{8,9},{9,10},{10,1... | collective-permute-start | bytes 968 | tf_op jit(solution)/shard_map/while/body/eval_jaxpr/ppermute | solution.py:11
  63.8 24.9 %collective-permute-start.3 = (s32[4,20]{1,0:T(4,128)S(1)}, s32[4,20]{1,0:T(4,128)S(1)}, u32[]{:S(2)}, u32[]{:S(2)}) collective-permute-start(s32[4,20]{1,0:T(4,128)S(1)} %get-tuple-element.407), channel_id=1, source_target_pairs={{0,255},{1,0},{2,1},{3,2},{4,3},{5,4},{6,5},{7,6},{8,7},{9,8},{10,... | collective-permute-start | bytes 968 | tf_op jit(solution)/shard_map/while/body/eval_jaxpr/ppermute | solution.py:11
  99.0 31.7 %collective-permute-start = (bf16[4,20,128,128]{3,2,1,0:T(8,128)(2,1)}, bf16[4,20,128,128]{3,2,1,0:T(8,128)(2,1)}, u32[]{:S(2)}, u32[]{:S(2)}) collective-permute-start(bf16[4,20,128,128]{3,2,1,0:T(8,128)(2,1)} %get-tuple-element.404), channel_id=1, source_target_pairs={{0,1},{1,2},{2,3},{3,4},{4,5},{5,6},{6,7},{7,8},{8,9},{9,10},{10,1... | collective-permute-start | bytes 7864328 | tf_op jit(solution)/shard_map/while/body/eval_jaxpr/ppermute | solution.py:11
  99.0 38.9 %collective-permute-start.2 = (bf16[4,20,128,128]{3,2,1,0:T(8,128)(2,1)}, bf16[4,20,128,128]{3,2,1,0:T(8,128)(2,1)S(1)}, u32[]{:S(2)}, u32[]{:S(2)}) collective-permute-start(bf16[4,20,128,128]{3,2,1,0:T(8,128)(2,1)} %get-tuple-element.406), channel_id=1, source_target_pairs={{0,255},{1,0},{2,1},{3,2},{4,3},{5,4},{6,5},{7,6},{8,7},{9,8},{10,... | collective-permute-start | bytes 7864328 | tf_op jit(solution)/shard_map/while/body/eval_jaxpr/ppermute | solution.py:11
  110.9 17.0 %collective-permute-start.1 = (s32[4,20]{1,0:T(4,128)S(1)}, s32[4,20]{1,0:T(4,128)S(1)}, u32[]{:S(2)}, u32[]{:S(2)}) collective-permute-start(s32[4,20]{1,0:T(4,128)S(1)} %get-tuple-element.405), channel_id=1, source_target_pairs={{0,1},{1,2},{2,3},{3,4},{4,5},{5,6},{6,7},{7,8},{8,9},{9,10},{10,1... | collective-permute-start | bytes 968 | tf_op jit(solution)/shard_map/while/body/eval_jaxpr/ppermute | solution.py:11
  110.9 19.8 %collective-permute-start.3 = (s32[4,20]{1,0:T(4,128)S(1)}, s32[4,20]{1,0:T(4,128)S(1)}, u32[]{:S(2)}, u32[]{:S(2)}) collective-permute-start(s32[4,20]{1,0:T(4,128)S(1)} %get-tuple-element.407), channel_id=1, source_target_pairs={{0,255},{1,0},{2,1},{3,2},{4,3},{5,4},{6,5},{7,6},{8,7},{9,8},{10,... | collective-permute-start | bytes 968 | tf_op jit(solution)/shard_map/while/body/eval_jaxpr/ppermute | solution.py:11
where the time goes:
time: 488 us; the launch traced here: 485 us
  local copies, waits for them, and re-layouts  181 us (37%)
  matrix products  105 us (22%)
  blocking collectives  94.9 us (19%)
  waiting for transfers between devices  53.1 us (11%)
  starting transfers between devices  44.6 us (9%)
    psum x1, blocking collectives, shards(): total_trace = lax.psum(jnp.sum(traces), ('blk', 'grp'))  94.9 us
    dot_general x4, local copies, waits for them, and re-layouts, one_row(): jnp.einsum('tus,tubc->tsbc', routing, far_tiles, preferred_element_type=j...  78.1 us
    dot_general x4, matrix products, one_row(): jnp.einsum('tus,tubc->tsbc', routing, far_tiles, preferred_element_type=j...  77.5 us
    ppermute x12, waiting for transfers between devices, shifted(): lax.ppermute(shard, axis, [(i, (i + by) % size) for i in range(size)])  53.1 us
    gather x4, local copies, waits for them, and re-layouts, one_row(): far_tiles = row_tiles[position]  50.7 us
    ppermute x12, starting transfers between devices, shifted(): lax.ppermute(shard, axis, [(i, (i + by) % size) for i in range(size)])  44.6 us
    dot_general x4, matrix products, one_row(): jnp.einsum('tab,tsbc->sac', own_tiles, panel, preferred_element_type=jnp....  27.4 us
    while x12, local copies, waits for them, and re-layouts  15.1 us
  transfers between devices with their start and end apart: 12, of which 6 were waited for; matrix products, arithmetic and copies ran while one was open for 4% of the time, Pallas kernels for 0%

commit v1 on v0

v1 whole, which is shorter than its diff:
```python
import functools

import jax
import jax.numpy as jnp
from jax import lax
from jax.experimental import pallas as pl
from jax.experimental.pallas import tpu as pltpu
from jax.sharding import PartitionSpec as P

REACH = 12
R = 4
BS = 128
COLS = 2 * REACH + R
MESH = pl.DeviceIdType.MESH


def spread_kernel(pos_ref, tiles_ref, dense_ref):
    dense_ref[...] = jnp.zeros_like(dense_ref)
    slots = tiles_ref.shape[1]
    for r in range(R):
        def place(s, carry, r=r):
            p = pos_ref[r, s]

            @pl.when(p >= 0)
            def _():
                dense_ref[r, p] = tiles_ref[r, s]

            return carry

        lax.fori_loop(0, slots, place, 0)


def square_kernel(n_blk, n_grp, pos_ref, own, square_ref, trace_ref,
                  out1, out2, out3, in1, in2, in3, acc, send_sem, recv_sem):
    n = n_blk * n_grp
    me = lax.axis_index("blk") * n_grp + lax.axis_index("grp")
    odd = lax.rem(me, 2)
    even = 1 - odd
    sign = 2 * odd - 1

    def dev(offset):
        d = lax.rem(me + offset + n, n)
        return (d // n_grp, lax.rem(d, n_grp))

    partner = dev(-sign)
    across = dev(sign)
    onward = dev(-2 * sign)
    behind = dev(2 * sign)

    barrier = pltpu.get_barrier_semaphore()
    for d in (partner, across, onward, behind):
        pl.semaphore_signal(barrier, inc=1, device_id=d, device_id_type=MESH)

    zero = jnp.zeros((BS, BS), jnp.bfloat16)
    for buf, delta, left in ((out1, 1, even), (out2, 2, even), (out3, 3, even),
                             (in1, 1, odd), (in2, 2, odd), (in3, 3, odd)):
        for rho in range(R - 1):
            row = left * rho + (1 - left) * (R - 1 - rho)
            first = left * (25 - 4 * delta + rho)
            for e in range(R - 1 - rho):
                buf[row, first + e] = zero
    pl.semaphore_wait(barrier, 4)

    def send(k, rho, src, src_left, length, dst, device, left):
        row = left * rho + (1 - left) * (R - 1 - rho)
        first = left * src_left + (1 - left) * (R - 1 - rho)
        to = (1 - left) * (R - 1 - rho)
        return pltpu.make_async_remote_copy(
            src_ref=src.at[row, pl.ds(first, length)],
            dst_ref=dst.at[row, pl.ds(to, length)],
            send_sem=send_sem.at[k, rho],
            recv_sem=recv_sem.at[k, rho],
            device_id=device,
            device_id_type=MESH,
        )

    def arrival(k, rho, buf, delta, left):
        length = 25 - 4 * delta + rho
        row = left * rho + (1 - left) * (R - 1 - rho)
        to = (1 - left) * (R - 1 - rho)
        here = buf.at[row, pl.ds(to, length)]
        return pltpu.make_async_copy(here, here, recv_sem.at[k, rho])

    sends = []

    def start(*args):
        c = send(*args)
        c.start()
        sends.append(c)

    order = (3, 2, 1, 0)
    for rho in order:
        start(0, rho, own, 4, 21 + rho, out1, across, odd)
    for rho in order:
        start(1, rho, own, 8, 17 + rho, out2, onward, even)
    for rho in order:
        start(3, rho, own, 4, 21 + rho, in1, partner, even)

    def product(buf, cols, left, delta, first=False):
        a0 = REACH + 4 * delta * (1 - 2 * left)
        c0 = (1 - left) * 4 * delta

        def step(t, carry):
            c = 2 * t
            lhs = jnp.concatenate([own[:, a0 + r].reshape(R * BS, BS) for r in range(R)], axis=1)
            rhs = jnp.concatenate([buf[:, c].reshape(R * BS, BS), buf[:, c + 1].reshape(R * BS, BS)], axis=1)
            res = jnp.dot(lhs, rhs, preferred_element_type=jnp.float32)
            for h in range(2):
                part = res[:, h * BS:(h + 1) * BS].reshape(R, BS, BS)
                if first:
                    acc[:, c0 + c + h] = part
                else:
                    acc[:, c0 + c + h] += part
            return carry

        lax.fori_loop(0, cols // 2, step, 0)

    product(own, 28, even, 0, first=True)
    for rho in order:
        arrival(3, rho, in1, 1, odd).wait()
    product(in1, 24, odd, 1)
    for rho in order:
        arrival(0, rho, out1, 1, even).wait()
        start(2, rho, out1, 8, 13 + rho, out3, onward, even)
        start(4, rho, out1, 4, 17 + rho, in2, partner, even)
        arrival(1, rho, out2, 2, even).wait()
        start(5, rho, out2, 4, 13 + rho, in3, partner, even)
    product(out2, 20, even, 2)
    product(out1, 24, even, 1)
    for rho in order:
        arrival(5, rho, in3, 3, odd).wait()
    product(in3, 16, odd, 3)
    for rho in order:
        arrival(4, rho, in2, 2, odd).wait()
    product(in2, 20, odd, 2)
    for rho in order:
        arrival(2, rho, out3, 3, even).wait()
    product(out3, 16, even, 3)

    for r in range(R):
        def take(s, carry, r=r):
            p = pos_ref[r, s]
            tile = acc[r, jnp.maximum(p, 0)]
            square_ref[r, s] = jnp.where(p >= 0, tile, 0.0).astype(jnp.bfloat16)
            return carry

        lax.fori_loop(0, square_ref.shape[1], take, 0)

    diagonal = sum(acc[r, REACH + r] for r in range(R))
    rows = lax.broadcasted_iota(jnp.int32, (BS, BS), 0)
    lanes = lax.broadcasted_iota(jnp.int32, (BS, BS), 1)
    diagonal = jnp.where(rows == lanes, diagonal, 0.0)
    trace_ref[...] = jnp.sum(diagonal.reshape(BS // 8, 8, BS), axis=0)

    for c in sends:
        c.wait_send()


def shards(tiles, columns, n_blk, n_grp):
    n = n_blk * n_grp
    all_rows = n * R
    me = lax.axis_index("blk") * n_grp + lax.axis_index("grp")
    pos = jnp.where(columns >= 0, jnp.mod(columns - me * R + REACH, all_rows), -1)
    dense = pl.pallas_call(
        spread_kernel,
        out_shape=jax.ShapeDtypeStruct((R, COLS, BS, BS), jnp.bfloat16),
        in_specs=[pl.BlockSpec(memory_space=pltpu.SMEM), pl.BlockSpec(memory_space=pltpu.VMEM)],
        out_specs=pl.BlockSpec(memory_space=pltpu.VMEM),
    )(pos, tiles)
    piece = lambda delta: pltpu.VMEM((R, COLS - 4 * delta, BS, BS), jnp.bfloat16)
    square, partial = pl.pallas_call(
        functools.partial(square_kernel, n_blk, n_grp),
        out_shape=(
            jax.ShapeDtypeStruct(tiles.shape, jnp.bfloat16),
            jax.ShapeDtypeStruct((8, BS), jnp.float32),
        ),
        in_specs=[pl.BlockSpec(memory_space=pltpu.SMEM), pl.BlockSpec(memory_space=pltpu.VMEM)],
        out_specs=(pl.BlockSpec(memory_space=pltpu.VMEM), pl.BlockSpec(memory_space=pltpu.VMEM)),
        scratch_shapes=[
            piece(1), piece(2), piece(3), piece(1), piece(2), piece(3),
            pltpu.VMEM((R, COLS, BS, BS), jnp.float32),
            pltpu.SemaphoreType.DMA((6, R)),
            pltpu.SemaphoreType.DMA((6, R)),
        ],
        compiler_params=pltpu.CompilerParams(
            collective_id=0, has_side_effects=True, vmem_limit_bytes=56 * 2**20
        ),
    )(pos, dense)
    total = lax.psum(jnp.sum(partial), ("blk", "grp"))
    return square, total / (all_rows * BS)


def solution(mesh):
    n_blk, n_grp = mesh.shape["blk"], mesh.shape["grp"]
    return jax.shard_map(
        functools.partial(shards, n_blk=n_blk, n_grp=n_grp),
        mesh=mesh,
        in_specs=(P(("blk", "grp"), None, None, None), P(("blk", "grp"), None)),
        out_specs=(P(("blk", "grp"), None, None, None), P()),
        check_vma=False,
    )
```

time: 488 us -> 189 us (0.39)
  local copies, waits for them, and re-layouts: 181 us -> 3.56 us
  matrix products: 105 us -> 0 us
  Pallas kernels: 0 us -> 98.8 us
  waiting for transfers between devices: 53.1 us -> 0 us
  starting transfers between devices: 44.6 us -> 0 us
  blocking collectives: 94.9 us -> 81.2 us
    dot_general x8 -> x0, matrix products: 105 us -> none  [the longest x4 77.5 us: one_row(): jnp.einsum('tus,tubc->tsbc', routing, far_tiles, preferred_element_type=j...]
    pallas_call x0 -> x2, Pallas kernels: none -> 98.8 us  [the longest x1 93.5 us: shards(): pl.pallas_call(functools.partial(square_kernel, n_blk, n_grp), out_shape=...]
    dot_general x4 -> x0, local copies, waits for them, and re-layouts: 78.1 us -> none  [one_row(): jnp.einsum('tus,tubc->tsbc', routing, far_tiles, preferred_element_type=j...]
    ppermute x12 -> x0, waiting for transfers between devices: 53.1 us -> none  [shifted(): lax.ppermute(shard, axis, [(i, (i + by) % size) for i in range(size)])]
    gather x8 -> x0, local copies, waits for them, and re-layouts: 52.9 us -> none  [the longest x4 50.7 us: one_row(): far_tiles = row_tiles[position]]
    ppermute x12 -> x0, starting transfers between devices: 44.6 us -> none  [shifted(): lax.ppermute(shard, axis, [(i, (i + by) % size) for i in range(size)])]
    dynamic_update_slice x24 -> x0, local copies, waits for them, and re-layouts: 23.6 us -> none  [the longest x3 10.7 us: advance(): lax.dynamic_update_index_in_dim(tile_acc, lower_piece[0], below_slot, 0)]
    while x12 -> x0, local copies, waits for them, and re-layouts: 15.1 us -> none
  transfers between devices with their start and end apart: 12 -> 0, of which waited for: 6 -> 0; matrix products, arithmetic and copies ran while one was open for 4% -> 0% of each run, Pallas kernels for 0% -> 0%
where the time goes in v1:
time: 189 us
  Pallas kernels  98.8 us (52%)
  blocking collectives  81.2 us (43%)
  local copies, waits for them, and re-layouts  3.56 us (2%)
  other arithmetic  2.56 us (1%)
  between operations  2.43 us (1%)
    pallas_call x1, Pallas kernels, shards(): pl.pallas_call(functools.partial(square_kernel, n_blk, n_grp), out_shape=...  93.5 us
    psum x1, blocking collectives, shards(): total = lax.psum(jnp.sum(partial), ('blk', 'grp'))  81.2 us
    pallas_call x1, Pallas kernels, shards(): pl.pallas_call(spread_kernel, out_shape=jax.ShapeDtypeStruct((R, COLS, BS...  5.27 us

profile of v1, /device:TPU:1, one launch (start us, length us, event | category | flops | bytes accessed | tf_op | source)
XLA Modules:
  0.0 188.6 jit_solution(4847838229714773968)
XLA Ops:
  0.6 1.3 fusion.1.pos_ref
  1.9 5.3 %shard_map.41.own = bf16[4,28,128,128]{3,2,1,0:T(8,128)(2,1)} custom-call(s32[4,20]{1,0:T(4,128)} %fusion.1.pos_ref, bf16[4,20,128,128]{3,2,1,0:T(8,128)(2,1)} %tiles_ref.1), custom_call_target="tpu_custom_call" | custom-call | tf_op jit(solution)/shard_map/pallas_call | solution.py:164
  7.2 93.5 %shard_map.42 = (bf16[4,20,128,128]{3,2,1,0:T(8,128)(2,1)}, f32[8,128]{1,0:T(8,128)}) custom-call(s32[4,20]{1,0:T(4,128)} %fusion.1.pos_ref, bf16[4,28,128,128]{3,2,1,0:T(8,128)(2,1)} %shard_map.41.own), custom_call_target="tpu_custom_call" | custom-call | tf_op jit(solution)/shard_map/pallas_call | solution.py:171
  100.7 1.3 reduce_sum.9
  102.0 81.2 %psum.7 = f32[]{:T(128)} all-reduce(f32[]{:T(128)} %reduce_sum.9), channel_id=1, replica_groups=mesh['blk'=16,'grp'=16] {'blk','grp'}, use_global_device_ids=true, to_apply=%region_1.2 | all-reduce | flops 1 | bytes 8 | tf_op jit(solution)/shard_map/psum | solution.py:189
  183.9 3.6 %copy.5 = bf16[4,20,128,128]{3,2,1,0:T(8,128)(2,1)} copy(bf16[4,20,128,128]{3,2,1,0:T(8,128)(2,1)} %get-tuple-element.8) | data formatting | bytes 5242880

commit v2 on v1

v2 whole, which is shorter than its diff:
```python
import functools

import jax
import jax.numpy as jnp
from jax import lax
from jax.experimental import pallas as pl
from jax.experimental.pallas import tpu as pltpu
from jax.sharding import PartitionSpec as P

REACH = 12
R = 4
BS = 128
COLS = 2 * REACH + R
MESH = pl.DeviceIdType.MESH
X_CHIPS = 4
ORDER = (3, 2, 1, 0)


def xor_strides(n):
    strides = []
    stride = 2 * X_CHIPS
    while stride < n:
        strides.append(stride)
        stride *= 2
    return strides


def square_kernel(n_blk, n_grp, columns_ref, tiles, square_ref, trace_ref,
                  own, out1, out2, out3, in1, in2, in3, acc, sent, got,
                  send_sem, recv_sem, sum_send_sem, sum_recv_sem):
    n = n_blk * n_grp
    slots = tiles.shape[1]
    me = lax.axis_index("blk") * n_grp + lax.axis_index("grp")
    odd = lax.rem(me, 2)
    even = 1 - odd
    sign = 2 * odd - 1

    def coords(d):
        return (d // n_grp, lax.rem(d, n_grp))

    def dev(offset):
        return coords(lax.rem(me + offset + n, n))

    partner = dev(-sign)
    across = dev(sign)
    onward = dev(-2 * sign)
    behind = dev(2 * sign)

    x = lax.rem(me // 2, X_CHIPS)
    ring_to = coords(me + 2 * (lax.rem(x + sign + X_CHIPS, X_CHIPS) - x))
    ring_from = coords(me + 2 * (lax.rem(x - sign + X_CHIPS, X_CHIPS) - x))
    mirrors = [coords(me + w * (1 - 2 * lax.rem(me // w, 2))) for w in xor_strides(n)]

    barrier = pltpu.get_barrier_semaphore()
    greeted = [partner, across, onward, behind, ring_to, ring_from] + mirrors
    for d in greeted:
        pl.semaphore_signal(barrier, inc=1, device_id=d, device_id_type=MESH)

    zero = jnp.zeros((BS, BS), jnp.bfloat16)
    for buf, delta, left in ((out1, 1, even), (out2, 2, even), (out3, 3, even),
                             (in1, 1, odd), (in2, 2, odd), (in3, 3, odd)):
        for rho in range(R - 1):
            row = left * rho + (1 - left) * (R - 1 - rho)
            first = left * (25 - 4 * delta + rho)
            for e in range(R - 1 - rho):
                buf[row, first + e] = zero

    def position(r, s):
        column = columns_ref[r, s]
        p = column - me * R + REACH
        p = jnp.where(p < 0, p + n * R, p)
        p = jnp.where(p >= n * R, p - n * R, p)
        return jnp.where(column >= 0, p, -1)

    def spread(r):
        filled = [position(r, s) for s in range(slots)]

        def place(p, carry):
            s = 0
            for k, f in enumerate(filled):
                s = jnp.where(f == p, k + 1, s)
            tile = tiles[r, jnp.maximum(s - 1, 0)]
            own[r, p] = jnp.where(s > 0, tile, zero)
            return carry

        lax.fori_loop(0, COLS, place, 0)

    sends = []

    def start(k, rho, src, first, dst, to, length, device, left):
        row = left * rho + (1 - left) * (R - 1 - rho)
        c = pltpu.make_async_remote_copy(
            src_ref=src.at[row, pl.ds(left * first[0] + (1 - left) * first[1], length)],
            dst_ref=dst.at[row, pl.ds(left * to[0] + (1 - left) * to[1], length)],
            send_sem=send_sem.at[k, rho],
            recv_sem=recv_sem.at[k, rho],
            device_id=device,
            device_id_type=MESH,
        )
        c.start()
        sends.append(c)

    def arrived(k, rho, buf, to, length, left):
        row = left * rho + (1 - left) * (R - 1 - rho)
        here = buf.at[row, pl.ds(left * to[0] + (1 - left) * to[1], length)]
        pltpu.make_async_copy(here, here, recv_sem.at[k, rho]).wait()

    def send_out1(rho):
        start(0, rho, own, (4, 3 - rho), out1, (0, 3 - rho), 21 + rho, across, odd)

    def send_in1(rho):
        start(3, rho, own, (4, 3 - rho), in1, (0, 3 - rho), 21 + rho, partner, even)

    def send_out2(rho):
        start(1, rho, own, (8, 4), out2, (0, 4), 16, onward, even)

    def send_out2_trace(rho):
        start(6, rho, own, (24, 3 - rho), out2, (16, 3 - rho), rho + 1, onward, even)

    def send_out3(rho):
        start(2, rho, out1, (8, 3 - rho), out3, (0, 3 - rho), 13 + rho, onward, even)

    def send_in2(rho):
        start(4, rho, out1, (4, 3 - rho), in2, (0, 3 - rho), 17 + rho, partner, even)

    def send_in3(rho):
        start(5, rho, out2, (4, 3 - rho), in3, (0, 3 - rho), 13 + rho, partner, even)

    def have_out1(rho):
        arrived(0, rho, out1, (0, 3 - rho), 21 + rho, even)

    def have_out2(rho):
        arrived(1, rho, out2, (0, 4), 16, even)

    def have_out2_trace(rho):
        arrived(6, rho, out2, (16, 3 - rho), rho + 1, even)

    def have_out3(rho):
        arrived(2, rho, out3, (0, 3 - rho), 13 + rho, even)

    def have_in1(rho):
        arrived(3, rho, in1, (0, 3 - rho), 21 + rho, odd)

    def have_in2(rho):
        arrived(4, rho, in2, (0, 3 - rho), 17 + rho, odd)

    def have_in3(rho):
        arrived(5, rho, in3, (0, 3 - rho), 13 + rho, odd)

    def pass_on(j, src, device):
        c = pltpu.make_async_remote_copy(
            src_ref=src,
            dst_ref=got.at[j],
            send_sem=sum_send_sem.at[j],
            recv_sem=sum_recv_sem.at[j],
            device_id=device,
            device_id_type=MESH,
        )
        c.start()
        sends.append(c)

    def received(j):
        pltpu.make_async_copy(got.at[j], got.at[j], sum_recv_sem.at[j]).wait()

    def product(buf, lo, hi, left, delta, first=False):
        a0 = REACH + 4 * delta * (1 - 2 * left)
        c0 = (1 - left) * 4 * delta

        def step(t, carry):
            c = 2 * t
            lhs = jnp.concatenate([own[:, a0 + r].reshape(R * BS, BS) for r in range(R)], axis=1)
            rhs = jnp.concatenate([buf[:, c].reshape(R * BS, BS), buf[:, c + 1].reshape(R * BS, BS)], axis=1)
            res = jnp.dot(lhs, rhs, preferred_element_type=jnp.float32)
            for h in range(2):
                part = res[:, h * BS:(h + 1) * BS].reshape(R, BS, BS)
                if first:
                    acc[:, c0 + c + h] = part
                else:
                    acc[:, c0 + c + h] += part
            return carry

        lax.fori_loop(lo // 2, hi // 2, step, 0)

    def spread_for_out1(rho):
        spread(odd * rho + even * (R - 1 - rho))

    spread_for_out1(3)
    pl.semaphore_wait(barrier, len(greeted))
    spread_for_out1(2)
    send_out1(3)
    spread_for_out1(1)
    send_out1(2)
    spread_for_out1(0)
    send_out1(1)
    for rho in (3, 2):
        send_in1(rho)
    send_out1(0)
    for rho in ORDER:
        send_out2_trace(rho)
    for rho in (1, 0):
        send_in1(rho)

    product(own, 0, 28, even, 0, first=True)
    for rho in ORDER:
        have_in1(rho)
    product(in1, 0, 24, odd, 1)

    for rho in ORDER:
        have_out1(rho)
        send_in2(rho)
        if rho == 1:
            for later in ORDER:
                send_out2(later)
    for rho in ORDER:
        send_out3(rho)
    product(out1, 0, 24, even, 1)
    for rho in ORDER:
        have_out2_trace(rho)
    for rho in ORDER:
        have_in2(rho)

    total = sum(acc[r, REACH + r] for r in range(R))
    for r in range(R):
        a = [out1[even * r + odd * q, even * (16 + q) + odd * (4 + r)] for q in range(R)]
        b = [in1[even * q + odd * r, even * (4 + r) + odd * (16 + q)] for q in range(R)]
        total += 2.0 * jnp.dot(
            jnp.concatenate(a, axis=1), jnp.concatenate(b, axis=0), preferred_element_type=jnp.float32
        )
    for r in range(R):
        a = [out1[even * r + odd * q, even * (20 + q) + odd * r] for q in range(r + 1)]
        b = [in2[even * q + odd * r, even * r + odd * (16 + q)] for q in range(r + 1)]
        a += [out2[even * r + odd * q, even * (16 + q) + odd * r] for q in range(r + 1)]
        b += [in1[even * q + odd * r, even * r + odd * (20 + q)] for q in range(r + 1)]
        total += jnp.dot(
            jnp.concatenate(a, axis=1), jnp.concatenate(b, axis=0), preferred_element_type=jnp.float32
        )
    rows = lax.broadcasted_iota(jnp.int32, (BS, BS), 0)
    lanes = lax.broadcasted_iota(jnp.int32, (BS, BS), 1)
    total = jnp.where(rows == lanes, total, 0.0)
    sent[0] = jnp.sum(total.reshape(BS // 8, 8, BS), axis=0)

    product(in2, 0, 4, odd, 2)
    pass_on(0, sent.at[0], partner)
    product(in2, 4, 12, odd, 2)
    received(0)
    sent[1] = sent[0] + got[0]
    product(in2, 12, 16, odd, 2)
    pass_on(1, sent.at[1], ring_to)
    product(in2, 16, 20, odd, 2)
    received(1)
    pass_on(2, got.at[1], ring_to)
    have_out2(3)
    send_in3(3)
    received(2)
    pass_on(3, got.at[2], ring_to)
    have_out2(2)
    send_in3(2)
    received(3)
    sent[4] = (sent[1] + got[2]) + (got[1] + got[3])
    have_out2(1)
    send_in3(1)
    last = 4 + len(mirrors)
    work = [
        lambda: (have_out2(0), send_in3(0)),
        lambda: product(out2, 0, 10, even, 2),
        lambda: product(out2, 10, 20, even, 2),
        lambda: [have_in3(rho) for rho in ORDER],
        lambda: product(in3, 0, 6, odd, 3),
        lambda: product(in3, 6, 12, odd, 3),
        lambda: product(in3, 12, 16, odd, 3),
    ]
    for j, mirror in enumerate(mirrors):
        pass_on(4 + j, sent.at[4 + j], mirror)
        if work:
            work.pop(0)()
        received(4 + j)
        sent[5 + j] = sent[4 + j] + got[4 + j]
        if work:
            work.pop(0)()
    for w in work:
        w()
    trace_ref[0, 0] = jnp.sum(sent[last]) * (1.0 / (n * R * BS))

    for rho in ORDER:
        have_out3(rho)
        row = even * rho + odd * (R - 1 - rho)
        top = odd * (R - 1 - rho)
        a0 = REACH + 12 * (1 - 2 * even) + row
        m = rho + 1
        begin = odd * (1 if rho < 2 else 0)
        c0 = odd * 12

        def step(t, carry, rho=rho, row=row, top=top, a0=a0, m=m, c0=c0):
            c = 2 * t
            lhs = own[pl.ds(top, m), a0].reshape(m * BS, BS)
            rhs = jnp.concatenate([out3[row, c], out3[row, c + 1]], axis=1)
            res = jnp.dot(lhs, rhs, preferred_element_type=jnp.float32)
            for h in range(2):
                acc[pl.ds(top, m), c0 + c + h] += res[:, h * BS:(h + 1) * BS].reshape(m, BS, BS)
            return carry

        lax.fori_loop(begin, begin + (7 if rho < 2 else 8), step, 0)
        done = even * rho + odd * (R - 1 - rho)

        def take(s, carry, done=done):
            p = position(done, s)
            tile = acc[done, jnp.clip(p, 0, COLS - 1)]
            square_ref[done, s] = jnp.where(p >= 0, tile, 0.0).astype(jnp.bfloat16)
            return carry

        lax.fori_loop(0, slots, take, 0)

    for c in sends:
        c.wait_send()


def shards(tiles, columns, n_blk, n_grp):
    n = n_blk * n_grp
    slots = tiles.shape[1]
    steps = 5 + len(xor_strides(n))
    piece = lambda delta: pltpu.VMEM((R, COLS - 4 * delta, BS, BS), jnp.bfloat16)
    square, trace_mean = pl.pallas_call(
        functools.partial(square_kernel, n_blk, n_grp),
        out_shape=(
            jax.ShapeDtypeStruct(tiles.shape, jnp.bfloat16),
            jax.ShapeDtypeStruct((1, 1), jnp.float32),
        ),
        in_specs=[
            pl.BlockSpec(memory_space=pltpu.SMEM),
            pl.BlockSpec(memory_space=pltpu.VMEM),
        ],
        out_specs=(pl.BlockSpec(memory_space=pltpu.VMEM), pl.BlockSpec(memory_space=pltpu.SMEM)),
        scratch_shapes=[
            piece(0),
            piece(1), piece(2), piece(3), piece(1), piece(2), piece(3),
            pltpu.VMEM((R, COLS, BS, BS), jnp.float32),
            pltpu.VMEM((steps, 8, BS), jnp.float32),
            pltpu.VMEM((steps, 8, BS), jnp.float32),
            pltpu.SemaphoreType.DMA((7, R)),
            pltpu.SemaphoreType.DMA((7, R)),
            pltpu.SemaphoreType.DMA((steps,)),
            pltpu.SemaphoreType.DMA((steps,)),
        ],
        compiler_params=pltpu.CompilerParams(
            collective_id=0, has_side_effects=True, vmem_limit_bytes=36 * 2**20
        ),
    )(columns, tiles)
    return square, trace_mean[0, 0]


def solution(mesh):
    n_blk, n_grp = mesh.shape["blk"], mesh.shape["grp"]
    return jax.shard_map(
        functools.partial(shards, n_blk=n_blk, n_grp=n_grp),
        mesh=mesh,
        in_specs=(P(("blk", "grp"), None, None, None), P(("blk", "grp"), None)),
        out_specs=(P(("blk", "grp"), None, None, None), P()),
        check_vma=False,
    )
```

time: 189 us -> 126 us (0.67)
  the two profiles are of different devices: /device:TPU:1 before, /device:TPU:30 now
where the time goes in v2:
time: 126 us
  Pallas kernels  119 us (94%)
  local copies, waits for them, and re-layouts  3.91 us (3%)
  between operations  2.41 us (2%)
    pallas_call x1, Pallas kernels, shards(): pl.pallas_call(functools.partial(square_kernel, n_blk, n_grp), out_shape=...  119 us
    unnamed x5, local copies, waits for them, and re-layouts  3.91 us

profile of v2, /device:TPU:30, one launch (start us, length us, event | category | flops | bytes accessed | tf_op | source)
XLA Modules:
  0.0 125.8 jit_solution(4624998811700804952)
XLA Ops:
  0.6 0.0 copy-start
  0.6 1.7 %copy-done = bf16[4,20,128,128]{3,2,1,0:T(8,128)(2,1)S(1)} copy-done((bf16[4,20,128,128]{3,2,1,0:T(8,128)(2,1)S(1)}, bf16[4,20,128,128]{3,2,1,0:T(8,128)(2,1)}, u32[]{:S(2)}) %copy-start) | copy-done | bytes 2621464
  2.4 0.0 copy-start.1
  2.4 0.7 copy-done.1
  3.1 119.5 %shard_map.41 = (bf16[4,20,128,128]{3,2,1,0:T(8,128)(2,1)S(1)}, f32[1,1]{1,0:T(1,128)}) custom-call(s32[4,20]{1,0:T(4,128)S(1)} %copy-done.1, bf16[4,20,128,128]{3,2,1,0:T(8,128)(2,1)S(1)} %copy-done), custom_call_target="tpu_custom_call" | custom-call | tf_op jit(solution)/shard_map/pallas_call | solution.py:322
  122.5 1.5 %copy.6 = bf16[4,20,128,128]{3,2,1,0:T(8,128)(2,1)} copy(bf16[4,20,128,128]{3,2,1,0:T(8,128)(2,1)S(1)} %get-tuple-element.8) | data formatting | bytes 5242880
Async XLA Ops:
  0.6 1.7 %copy-start = (bf16[4,20,128,128]{3,2,1,0:T(8,128)(2,1)S(1)}, bf16[4,20,128,128]{3,2,1,0:T(8,128)(2,1)}, u32[]{:S(2)}) copy-start(bf16[4,20,128,128]{3,2,1,0:T(8,128)(2,1)} %tiles.1) | copy-start | bytes 7864324
  2.4 0.7 copy-start.1

commit v3 on v2

--- a/solution.py
+++ b/solution.py
@@ -12,22 +12,21 @@
 BS = 128
 COLS = 2 * REACH + R
 MESH = pl.DeviceIdType.MESH
-X_CHIPS = 4
 ORDER = (3, 2, 1, 0)
 
 
-def xor_strides(n):
-    strides = []
-    stride = 2 * X_CHIPS
-    while stride < n:
-        strides.append(stride)
-        stride *= 2
-    return strides
-
-
-def square_kernel(n_blk, n_grp, columns_ref, tiles, square_ref, trace_ref,
-                  own, out1, out2, out3, in1, in2, in3, acc, sent, got,
-                  send_sem, recv_sem, sum_send_sem, sum_recv_sem):
+def xor_groups(n):
+    groups = []
+    for bits in ((2, 4), (8, 64, 128), (16, 32)):
+        bits = [w for w in bits if w < n]
+        if bits:
+            groups.append([sum(w for i, w in enumerate(bits) if k >> i & 1) for k in range(1, 2 ** len(bits))])
+    return groups
+
+
+def square_kernel(n_blk, n_grp, columns_hbm, tiles_hbm, square_ref, trace_ref,
+                  columns_ref, tiles, own, out1, out2, out3, in1, in2, in3, acc, sent, got,
+                  load_sem, send_sem, recv_sem, sum_send_sem, sum_recv_sem):
     n = n_blk * n_grp
     slots = tiles.shape[1]
     me = lax.axis_index("blk") * n_grp + lax.axis_index("grp")
@@ -35,6 +34,13 @@
     even = 1 - odd
     sign = 2 * odd - 1
 
+    loads = [
+        pltpu.make_async_copy(columns_hbm, columns_ref, load_sem.at[0]),
+        pltpu.make_async_copy(tiles_hbm, tiles, load_sem.at[1]),
+    ]
+    for c in loads:
+        c.start()
+
     def coords(d):
         return (d // n_grp, lax.rem(d, n_grp))
 
@@ -46,13 +52,19 @@
     onward = dev(-2 * sign)
     behind = dev(2 * sign)
 
-    x = lax.rem(me // 2, X_CHIPS)
-    ring_to = coords(me + 2 * (lax.rem(x + sign + X_CHIPS, X_CHIPS) - x))
-    ring_from = coords(me + 2 * (lax.rem(x - sign + X_CHIPS, X_CHIPS) - x))
-    mirrors = [coords(me + w * (1 - 2 * lax.rem(me // w, 2))) for w in xor_strides(n)]
+    def mirror(mask):
+        d = me
+        w = 1
+        while w < n:
+            if mask & w:
+                d += w * (1 - 2 * lax.rem(me // w, 2))
+            w *= 2
+        return coords(d)
+
+    groups = [[mirror(mask) for mask in group] for group in xor_groups(n)]
 
     barrier = pltpu.get_barrier_semaphore()
-    greeted = [partner, across, onward, behind, ring_to, ring_from] + mirrors
+    greeted = [partner, across, onward, behind] + sum(groups, [])
     for d in greeted:
         pl.semaphore_signal(barrier, inc=1, device_id=d, device_id_type=MESH)
 
@@ -85,7 +97,7 @@
 
         lax.fori_loop(0, COLS, place, 0)
 
-    sends = []
+    sends = {}
 
     def start(k, rho, src, first, dst, to, length, device, left):
         row = left * rho + (1 - left) * (R - 1 - rho)
@@ -98,7 +110,10 @@
             device_id_type=MESH,
         )
         c.start()
-        sends.append(c)
+        sends[k, rho] = c
+
+    def wait_sent(k, rho):
+        sends.pop((k, rho)).wait_send()
 
     def arrived(k, rho, buf, to, length, left):
         row = left * rho + (1 - left) * (R - 1 - rho)
@@ -157,7 +172,7 @@
             device_id_type=MESH,
         )
         c.start()
-        sends.append(c)
+        sends["sum", j] = c
 
     def received(j):
         pltpu.make_async_copy(got.at[j], got.at[j], sum_recv_sem.at[j]).wait()
@@ -184,9 +199,11 @@
     def spread_for_out1(rho):
         spread(odd * rho + even * (R - 1 - rho))
 
+    for c in loads:
+        c.wait()
     spread_for_out1(3)
+    spread_for_out1(2)
     pl.semaphore_wait(barrier, len(greeted))
-    spread_for_out1(2)
     send_out1(3)
     spread_for_out1(1)
     send_out1(2)
@@ -208,11 +225,8 @@
     for rho in ORDER:
         have_out1(rho)
         send_in2(rho)
-        if rho == 1:
-            for later in ORDER:
-                send_out2(later)
-    for rho in ORDER:
-        send_out3(rho)
+    send_out3(3)
+    send_out2(3)
     product(out1, 0, 24, even, 1)
     for rho in ORDER:
         have_out2_trace(rho)
@@ -241,47 +255,58 @@
 
     product(in2, 0, 4, odd, 2)
     pass_on(0, sent.at[0], partner)
-    product(in2, 4, 12, odd, 2)
+    product(in2, 4, 8, odd, 2)
     received(0)
     sent[1] = sent[0] + got[0]
-    product(in2, 12, 16, odd, 2)
-    pass_on(1, sent.at[1], ring_to)
-    product(in2, 16, 20, odd, 2)
-    received(1)
-    pass_on(2, got.at[1], ring_to)
-    have_out2(3)
-    send_in3(3)
-    received(2)
-    pass_on(3, got.at[2], ring_to)
-    have_out2(2)
-    send_in3(2)
-    received(3)
-    sent[4] = (sent[1] + got[2]) + (got[1] + got[3])
-    have_out2(1)
-    send_in3(1)
-    last = 4 + len(mirrors)
+    product(in2, 8, 10, odd, 2)
+    queue = [
+        lambda: send_out2(2),
+        lambda: send_out2(1),
+        lambda: (send_out2(0), send_out3(2), send_out3(1), send_out3(0)),
+    ]
     work = [
-        lambda: (have_out2(0), send_in3(0)),
-        lambda: product(out2, 0, 10, even, 2),
-        lambda: product(out2, 10, 20, even, 2),
-        lambda: [have_in3(rho) for rho in ORDER],
-        lambda: product(in3, 0, 6, odd, 3),
-        lambda: product(in3, 6, 12, odd, 3),
-        lambda: product(in3, 12, 16, odd, 3),
+        lambda: product(in2, 10, 18, odd, 2),
+        lambda: [(have_out2(rho), send_in3(rho)) for rho in (3, 2)],
+        lambda: [(have_out2(rho), send_in3(rho)) for rho in (1, 0)],
     ]
-    for j, mirror in enumerate(mirrors):
-        pass_on(4 + j, sent.at[4 + j], mirror)
-        if work:
-            work.pop(0)()
-        received(4 + j)
-        sent[5 + j] = sent[4 + j] + got[4 + j]
-        if work:
-            work.pop(0)()
-    for w in work:
-        w()
-    trace_ref[0, 0] = jnp.sum(sent[last]) * (1.0 / (n * R * BS))
-
-    for rho in ORDER:
+    fill = [lambda: product(in2, 18, 20, odd, 2)]
+    def add_up(j, at, group):
+        values = [sent[1 + j]]
+        for k in range(len(group)):
+            received(at + k)
+            values.append(got[at + k])
+        while len(values) > 1:
+            values = [values[i] + values[i + 1] for i in range(0, len(values), 2)]
+        sent[2 + j] = values[0]
+
+    before = [(2, 3), (1, 3), (1, 2)]
+    for rho in ORDER:
+        wait_sent(0, rho)
+        wait_sent(6, rho)
+    at = 1
+    for j, group in enumerate(groups):
+        wait_sent(*before[j])
+        for k, d in enumerate(group):
+            pass_on(at + k, sent.at[1 + j], d)
+        for q in queue[j:] if j == len(groups) - 1 else queue[j:j + 1]:
+            q()
+        for w in work[j:] if j == len(groups) - 1 else work[j:j + 1]:
+            w()
+        if j < len(groups) - 1:
+            add_up(j, at, group)
+            for f in fill[j:j + 1]:
+                f()
+        at += len(group)
+    last = 1 + len(groups)
+    product(out2, 0, 20, even, 2)
+    for rho in ORDER:
+        have_in3(rho)
+    product(in3, 0, 16, odd, 3)
+
+    for rho in ORDER:
+        if rho == 0:
+            add_up(len(groups) - 1, at - len(groups[-1]), groups[-1])
+            trace_ref[0, 0] = jnp.sum(sent[last]) * (1.0 / (n * R * BS))
         have_out3(rho)
         row = even * rho + odd * (R - 1 - rho)
         top = odd * (R - 1 - rho)
@@ -310,14 +335,14 @@
 
         lax.fori_loop(0, slots, take, 0)
 
-    for c in sends:
+    for c in sends.values():
         c.wait_send()
 
 
 def shards(tiles, columns, n_blk, n_grp):
     n = n_blk * n_grp
     slots = tiles.shape[1]
-    steps = 5 + len(xor_strides(n))
+    steps = 1 + sum(len(group) for group in xor_groups(n))
     piece = lambda delta: pltpu.VMEM((R, COLS - 4 * delta, BS, BS), jnp.bfloat16)
     square, trace_mean = pl.pallas_call(
         functools.partial(square_kernel, n_blk, n_grp),
@@ -326,16 +351,19 @@
             jax.ShapeDtypeStruct((1, 1), jnp.float32),
         ),
         in_specs=[
-            pl.BlockSpec(memory_space=pltpu.SMEM),
-            pl.BlockSpec(memory_space=pltpu.VMEM),
+            pl.BlockSpec(memory_space=pltpu.HBM),
+            pl.BlockSpec(memory_space=pltpu.HBM),
         ],
         out_specs=(pl.BlockSpec(memory_space=pltpu.VMEM), pl.BlockSpec(memory_space=pltpu.SMEM)),
         scratch_shapes=[
+            pltpu.SMEM(columns.shape, jnp.int32),
+            pltpu.VMEM(tiles.shape, jnp.bfloat16),
             piece(0),
             piece(1), piece(2), piece(3), piece(1), piece(2), piece(3),
             pltpu.VMEM((R, COLS, BS, BS), jnp.float32),
             pltpu.VMEM((steps, 8, BS), jnp.float32),
             pltpu.VMEM((steps, 8, BS), jnp.float32),
+            pltpu.SemaphoreType.DMA((2,)),
             pltpu.SemaphoreType.DMA((7, R)),
             pltpu.SemaphoreType.DMA((7, R)),
             pltpu.SemaphoreType.DMA((steps,)),
@@ -344,7 +372,7 @@
         compiler_params=pltpu.CompilerParams(
             collective_id=0, has_side_effects=True, vmem_limit_bytes=36 * 2**20
         ),
-    )(columns, tiles)
+    )(pltpu.with_memory_space_constraint(columns, pltpu.HBM), pltpu.with_memory_space_constraint(tiles, pltpu.HBM))
     return square, trace_mean[0, 0]
 
 

time: 126 us -> 103 us (0.82)
  the two profiles are of different devices: /device:TPU:30 before, /device:TPU:1 now
where the time goes in v3:
time: 103 us
  Pallas kernels  99.2 us (96%)
  between operations  2.33 us (2%)
  local copies, waits for them, and re-layouts  1.49 us (1%)
    pallas_call x1, Pallas kernels, shards(): pl.pallas_call(functools.partial(square_kernel, n_blk, n_grp), out_shape=...  99.2 us

profile of v3, /device:TPU:1, one launch (start us, length us, event | category | flops | bytes accessed | tf_op | source)
XLA Modules:
  0.0 103.0 jit_solution(17549810181768037037)
XLA Ops:
  0.6 99.2 %shard_map.41 = (bf16[4,20,128,128]{3,2,1,0:T(8,128)(2,1)S(1)}, f32[1,1]{1,0:T(1,128)}) custom-call(s32[4,20]{1,0:T(4,128)} %columns_hbm.1, bf16[4,20,128,128]{3,2,1,0:T(8,128)(2,1)} %tiles_hbm.1), custom_call_target="tpu_custom_call" | custom-call | tf_op jit(solution)/shard_map/pallas_call | solution.py:347
  99.9 1.5 %copy.6 = bf16[4,20,128,128]{3,2,1,0:T(8,128)(2,1)} copy(bf16[4,20,128,128]{3,2,1,0:T(8,128)(2,1)S(1)} %get-tuple-element.8) | data formatting | bytes 5242880

commit v4 on v3

--- a/solution.py
+++ b/solution.py
@@ -25,7 +25,8 @@
 
 
 def square_kernel(n_blk, n_grp, columns_hbm, tiles_hbm, square_ref, trace_ref,
-                  columns_ref, tiles, own, out1, out2, out3, in1, in2, in3, acc, sent, got,
+                  columns_ref, across_vmem, across_ref, tiles, own, raw3, raw2, raw1, raw0,
+                  out1, out2, out3, in1, in2, in3, acc, sent, got,
                   load_sem, send_sem, recv_sem, sum_send_sem, sum_recv_sem):
     n = n_blk * n_grp
     slots = tiles.shape[1]
@@ -69,7 +70,8 @@
         pl.semaphore_signal(barrier, inc=1, device_id=d, device_id_type=MESH)
 
     zero = jnp.zeros((BS, BS), jnp.bfloat16)
-    for buf, delta, left in ((out1, 1, even), (out2, 2, even), (out3, 3, even),
+    raw = {3: raw3, 2: raw2, 1: raw1, 0: raw0}
+    for buf, delta, left in ((out2, 2, even), (out3, 3, even),
                              (in1, 1, odd), (in2, 2, odd), (in3, 3, odd)):
         for rho in range(R - 1):
             row = left * rho + (1 - left) * (R - 1 - rho)
@@ -77,25 +79,30 @@
             for e in range(R - 1 - rho):
                 buf[row, first + e] = zero
 
-    def position(r, s):
-        column = columns_ref[r, s]
+    def position(columns, r, s):
+        column = columns[r, s]
         p = column - me * R + REACH
         p = jnp.where(p < 0, p + n * R, p)
         p = jnp.where(p >= n * R, p - n * R, p)
         return jnp.where(column >= 0, p, -1)
 
-    def spread(r):
-        filled = [position(r, s) for s in range(slots)]
+    def spread(columns, r, source, target, first, count):
+        filled = [position(columns, r, s) for s in range(slots)]
 
         def place(p, carry):
             s = 0
             for k, f in enumerate(filled):
-                s = jnp.where(f == p, k + 1, s)
-            tile = tiles[r, jnp.maximum(s - 1, 0)]
-            own[r, p] = jnp.where(s > 0, tile, zero)
-            return carry
-
-        lax.fori_loop(0, COLS, place, 0)
+                s = jnp.where(f == p + first, k + 1, s)
+            tile = source(jnp.maximum(s - 1, 0))
+            target[r, p] = jnp.where(s > 0, tile, zero)
+            return carry
+
+        def place_some(g, carry):
+            for e in range(4):
+                place(4 * g + e, carry)
+            return carry
+
+        lax.fori_loop(0, count // 4, place_some, 0)
 
     sends = {}
 
@@ -121,7 +128,16 @@
         pltpu.make_async_copy(here, here, recv_sem.at[k, rho]).wait()
 
     def send_out1(rho):
-        start(0, rho, own, (4, 3 - rho), out1, (0, 3 - rho), 21 + rho, across, odd)
+        c = pltpu.make_async_remote_copy(
+            src_ref=tiles_hbm.at[odd * rho + even * (R - 1 - rho)],
+            dst_ref=raw[rho],
+            send_sem=send_sem.at[0, rho],
+            recv_sem=recv_sem.at[0, rho],
+            device_id=across,
+            device_id_type=MESH,
+        )
+        c.start()
+        sends[0, rho] = c
 
     def send_in1(rho):
         start(3, rho, own, (4, 3 - rho), in1, (0, 3 - rho), 21 + rho, partner, even)
@@ -142,7 +158,9 @@
         start(5, rho, out2, (4, 3 - rho), in3, (0, 3 - rho), 13 + rho, partner, even)
 
     def have_out1(rho):
-        arrived(0, rho, out1, (0, 3 - rho), 21 + rho, even)
+        pltpu.make_async_copy(raw[rho], raw[rho], recv_sem.at[0, rho]).wait()
+        row = even * rho + odd * (R - 1 - rho)
+        spread(across_ref, row, lambda s: raw[rho][s], out1, odd * 4, COLS - 4)
 
     def have_out2(rho):
         arrived(1, rho, out2, (0, 4), 16, even)
@@ -196,25 +214,32 @@
 
         lax.fori_loop(lo // 2, hi // 2, step, 0)
 
-    def spread_for_out1(rho):
-        spread(odd * rho + even * (R - 1 - rho))
-
+    pl.semaphore_wait(barrier, len(greeted))
+    c = pltpu.make_async_remote_copy(
+        src_ref=columns_hbm,
+        dst_ref=across_vmem,
+        send_sem=send_sem.at[7, 0],
+        recv_sem=recv_sem.at[7, 0],
+        device_id=across,
+        device_id_type=MESH,
+    )
+    c.start()
+    sends[7, 0] = c
+    for rho in ORDER:
+        send_out1(rho)
     for c in loads:
         c.wait()
-    spread_for_out1(3)
-    spread_for_out1(2)
-    pl.semaphore_wait(barrier, len(greeted))
-    send_out1(3)
-    spread_for_out1(1)
-    send_out1(2)
-    spread_for_out1(0)
-    send_out1(1)
-    for rho in (3, 2):
-        send_in1(rho)
-    send_out1(0)
+    for rho in ORDER:
+        r = odd * rho + even * (R - 1 - rho)
+        spread(columns_ref, r, lambda s, r=r: tiles[r, s], own, 0, COLS)
+    pltpu.make_async_copy(across_vmem, across_vmem, recv_sem.at[7, 0]).wait()
+    c = pltpu.make_async_copy(across_vmem, across_ref, load_sem.at[2])
+    c.start()
+    c.wait()
     for rho in ORDER:
         send_out2_trace(rho)
-    for rho in (1, 0):
+    send_out2(3)
+    for rho in ORDER:
         send_in1(rho)
 
     product(own, 0, 28, even, 0, first=True)
@@ -224,9 +249,10 @@
 
     for rho in ORDER:
         have_out1(rho)
-        send_in2(rho)
+        if rho < 3:
+            send_in2(rho + 1)
     send_out3(3)
-    send_out2(3)
+    send_in2(0)
     product(out1, 0, 24, even, 1)
     for rho in ORDER:
         have_out2_trace(rho)
@@ -279,7 +305,7 @@
             values = [values[i] + values[i + 1] for i in range(0, len(values), 2)]
         sent[2 + j] = values[0]
 
-    before = [(2, 3), (1, 3), (1, 2)]
+    before = [(1, 3), (2, 3), (1, 2)]
     for rho in ORDER:
         wait_sent(0, rho)
         wait_sent(6, rho)
@@ -324,16 +350,27 @@
                 acc[pl.ds(top, m), c0 + c + h] += res[:, h * BS:(h + 1) * BS].reshape(m, BS, BS)
             return carry
 
-        lax.fori_loop(begin, begin + (7 if rho < 2 else 8), step, 0)
+        if rho < 2:
+            for t in range(7):
+                step(begin + t, 0)
+        else:
+            lax.fori_loop(0, 8, step, 0)
         done = even * rho + odd * (R - 1 - rho)
 
         def take(s, carry, done=done):
-            p = position(done, s)
+            p = position(columns_ref, done, s)
             tile = acc[done, jnp.clip(p, 0, COLS - 1)]
             square_ref[done, s] = jnp.where(p >= 0, tile, 0.0).astype(jnp.bfloat16)
             return carry
 
-        lax.fori_loop(0, slots, take, 0)
+        def take_some(g, carry, take=take):
+            for e in range(5):
+                take(5 * g + e, carry)
+            return carry
+
+        lax.fori_loop(0, slots // 5, take_some, 0)
+        for t in range(slots // 5 * 5, slots):
+            take(t, 0)
 
     for c in sends.values():
         c.wait_send()
@@ -357,20 +394,23 @@
         out_specs=(pl.BlockSpec(memory_space=pltpu.VMEM), pl.BlockSpec(memory_space=pltpu.SMEM)),
         scratch_shapes=[
             pltpu.SMEM(columns.shape, jnp.int32),
+            pltpu.VMEM(columns.shape, jnp.int32),
+            pltpu.SMEM(columns.shape, jnp.int32),
             pltpu.VMEM(tiles.shape, jnp.bfloat16),
             piece(0),
+        ] + [pltpu.VMEM(tiles.shape[1:], jnp.bfloat16)] * R + [
             piece(1), piece(2), piece(3), piece(1), piece(2), piece(3),
             pltpu.VMEM((R, COLS, BS, BS), jnp.float32),
             pltpu.VMEM((steps, 8, BS), jnp.float32),
             pltpu.VMEM((steps, 8, BS), jnp.float32),
-            pltpu.SemaphoreType.DMA((2,)),
-            pltpu.SemaphoreType.DMA((7, R)),
-            pltpu.SemaphoreType.DMA((7, R)),
+            pltpu.SemaphoreType.DMA((3,)),
+            pltpu.SemaphoreType.DMA((8, R)),
+            pltpu.SemaphoreType.DMA((8, R)),
             pltpu.SemaphoreType.DMA((steps,)),
             pltpu.SemaphoreType.DMA((steps,)),
         ],
         compiler_params=pltpu.CompilerParams(
-            collective_id=0, has_side_effects=True, vmem_limit_bytes=36 * 2**20
+            collective_id=0, has_side_effects=True, vmem_limit_bytes=40 * 2**20
         ),
     )(pltpu.with_memory_space_constraint(columns, pltpu.HBM), pltpu.with_memory_space_constraint(tiles, pltpu.HBM))
     return square, trace_mean[0, 0]

time: 103 us -> 101 us (0.981)
  the two profiles are of different devices: /device:TPU:1 before, /device:TPU:0 now
where the time goes in v4:
time: 101 us
  Pallas kernels  97.4 us (96%)
  between operations  2.33 us (2%)
  local copies, waits for them, and re-layouts  1.49 us (1%)
    pallas_call x1, Pallas kernels, shards(): pl.pallas_call(functools.partial(square_kernel, n_blk, n_grp), out_shape=...  97.4 us

profile of v4, /device:TPU:0, one launch (start us, length us, event | category | flops | bytes accessed | tf_op | source)
XLA Modules:
  0.0 101.3 jit_solution(13141335328707917827)
XLA Ops:
  0.6 97.4 %shard_map.41 = (bf16[4,20,128,128]{3,2,1,0:T(8,128)(2,1)S(1)}, f32[1,1]{1,0:T(1,128)}) custom-call(s32[4,20]{1,0:T(4,128)} %columns_hbm.1, bf16[4,20,128,128]{3,2,1,0:T(8,128)(2,1)} %tiles_hbm.1), custom_call_target="tpu_custom_call" | custom-call | tf_op jit(solution)/shard_map/pallas_call | solution.py:384
  98.1 1.5 %copy.6 = bf16[4,20,128,128]{3,2,1,0:T(8,128)(2,1)} copy(bf16[4,20,128,128]{3,2,1,0:T(8,128)(2,1)S(1)} %get-tuple-element.8) | data formatting | bytes 5242880
